TPU v7x, 128 devices: a whole 4x4x4 slice. The times are simulated.
128 devices in a mesh: row: 8 (over x, core), col: 16 (over z, y).
Axes of the slice: x: 4, y: 4, z: 4, core: 2. Of those that a mesh axis runs over, the one named last changes fastest.
Arguments:
- right_sides: bfloat16 [32768, 12288], P('row', 'col'), may hold values from -6 to 6
- factor_panels: bfloat16 [32768, 1024], P(('row', 'col')), may hold values from -0.1875 to 0.1875
- inverse_blocks: float32 [4, 256, 256], replicated, may hold values from -1 to 1, as said below
Outputs:
- solved_sides: float32 [32768, 12288], P('row', 'col')
Inputs may be any that keep to these rules, and one draw needn't show every extreme that they name: `inverse_blocks`: each block is unit lower triangular.
All inputs are finite; a program needn't handle non-finite values.
Results may differ from a plain program's by a relative error of at most 0.003.
Values may be sent and summed in bfloat16 or wider, within the bound.
No kernel may reach another device: no remote copies, remote signals or barrier semaphores. Data moves between devices by JAX's collectives and lax.ppermute only.
A program may use at most 192 MiB of HBM per device.

v0:
```python
import jax
import jax.numpy as jnp
from jax import lax
from jax.sharding import PartitionSpec as P


def from_root(value, axis, root):
    mine = lax.axis_index(axis) == root
    return lax.psum(jnp.where(mine, value, jnp.zeros_like(value)), axis)


def publish(solved, panel_num):
    return from_root(solved.astype(jnp.bfloat16), "row", panel_num)


def per_device(right_sides, factor_panels, inverse_blocks):
    panel_count = inverse_blocks.shape[0]
    panel_width = inverse_blocks.shape[1]
    row_index = lax.axis_index("row")
    current = right_sides.astype(jnp.float32)
    for panel_num in range(panel_count):
        leading = current[:panel_width]
        solved = jnp.dot(inverse_blocks[panel_num], leading, precision=lax.Precision.HIGHEST)
        shared = publish(solved, panel_num)
        columns = factor_panels[:, panel_num * panel_width : (panel_num + 1) * panel_width]
        update = jnp.dot(
            lax.all_gather(columns, "col", axis=0, tiled=True),
            shared,
            preferred_element_type=jnp.float32,
        )
        updated_first = jnp.where(row_index > panel_num, leading - update[:panel_width], leading)
        new_first = jnp.where(row_index == panel_num, solved, updated_first)
        current = jnp.concatenate([new_first, current[panel_width:] - update[panel_width:]], 0)
    return current


def solution(mesh):
    placed = (P("row", "col"), P(("row", "col"), None), P())
    return jax.shard_map(
        per_device, mesh=mesh, in_specs=placed, out_specs=P("row", "col"), check_vma=False
    )
```

profile of v0, /device:TPU:0, one launch (start us, length us, event | category | flops | bytes accessed | tf_op | source)
XLA Modules:
  0.0 335.0 jit_solution(2568119471155261356)
XLA Ops:
  7.4 2.3 convert_select_fusion.3
  9.7 0.0 all-gather.5.cloned.1.call-start
  9.8 1.9 fusion.14
  11.7 0.0 all-gather.7.cloned.1.call-start
  11.7 0.5 all-gather.7.cloned.1.call-update
  12.3 8.6 %convert_element_type.15 = f32[4096,768]{1,0:T(8,128)} convert(bf16[4096,768]{1,0:T(8,128)(2,1)} %param.3) | non-fusion elementwise | flops 3145728 | bytes 18874368 | tf_op jit(solution)/shard_map/convert_element_type | solution.py:20
  20.9 53.2 %all-reduce.5.cloned.1.call-done = bf16[256,768]{1,0:T(8,128)(2,1)} async-done(((bf16[256,768]{1,0:T(8,128)(2,1)}), bf16[256,768]{1,0:T(8,128)(2,1)}) %all-reduce.5.cloned.1.call-update) | async-done | bytes 393232 | tf_op jit(solution)/shard_map/psum | solution.py:9
  74.1 3.4 %convolution_bitcast_fusion.3 = f32[4096,768]{1,0:T(8,128)S(1)} fusion(bf16[4096,256]{1,0:T(8,128)(2,1)} %all-gather.5.cloned.1.call-done, bf16[256,768]{1,0:T(8,128)(2,1)} %all-reduce.5.cloned.1.call-done), kind=kOutput, calls=%fused_computation.8 | convolution fusion | flops 1610612736 | bytes 15073280 | tf_op jit(solution)/shard_map/dot_general | solution.py:26
  77.5 4.5 %copy-done = f32[4096,768]{1,0:T(8,128)} copy-done((f32[4096,768]{1,0:T(8,128)}, f32[4096,768]{1,0:T(8,128)S(1)}, u32[]{:S(2)}) %copy-start) | copy-done | bytes 12582936
  82.0 1.3 fusion
  83.3 1.6 convert_select_fusion.2
  85.0 0.0 all-gather.9.cloned.1.call-start
  85.0 0.5 all-gather.9.cloned.1.call-update
  85.6 20.7 %all-gather.7.cloned.1.call-done = bf16[4096,256]{1,0:T(8,128)(2,1)} async-done(((bf16[256,256]{1,0:T(8,128)(2,1)}), bf16[4096,256]{1,0:T(8,128)(2,1)}) %all-gather.7.cloned.1.call-update) | async-done | bytes 2097168 | tf_op jit(solution)/shard_map/all_gather | solution.py:27
  106.3 38.7 %all-reduce.7.cloned.1.call-done = bf16[256,768]{1,0:T(8,128)(2,1)} async-done(((bf16[256,768]{1,0:T(8,128)(2,1)}), bf16[256,768]{1,0:T(8,128)(2,1)}) %all-reduce.7.cloned.1.call-update) | async-done | bytes 393232 | tf_op jit(solution)/shard_map/psum | solution.py:9
  145.0 3.4 %convolution_bitcast_fusion.2 = f32[4096,768]{1,0:T(8,128)S(1)} fusion(bf16[4096,256]{1,0:T(8,128)(2,1)} %all-gather.7.cloned.1.call-done, bf16[256,768]{1,0:T(8,128)(2,1)} %all-reduce.7.cloned.1.call-done), kind=kOutput, calls=%fused_computation.7 | convolution fusion | flops 1610612736 | bytes 15073280 | tf_op jit(solution)/shard_map/dot_general | solution.py:26
  148.5 4.5 %copy-done.1 = f32[4096,768]{1,0:T(8,128)} copy-done((f32[4096,768]{1,0:T(8,128)}, f32[4096,768]{1,0:T(8,128)S(1)}, u32[]{:S(2)}) %copy-start.1) | copy-done | bytes 12582936
  153.0 0.1 fusion.1
  153.1 1.6 convert_select_fusion.1
  154.8 0.0 all-gather.11.cloned.1.call-start
  154.8 0.7 all-gather.11.cloned.1.call-update
  155.5 0.2 all-reduce.11.cloned.1.call-start
  155.8 59.4 %all-reduce.9.cloned.1.call-done = bf16[256,768]{1,0:T(8,128)(2,1)} async-done(((bf16[256,768]{1,0:T(8,128)(2,1)}), bf16[256,768]{1,0:T(8,128)(2,1)}) %all-reduce.9.cloned.1.call-update) | async-done | bytes 393232 | tf_op jit(solution)/shard_map/psum | solution.py:9
  215.2 3.4 %convolution_bitcast_fusion.1 = f32[4096,768]{1,0:T(8,128)S(1)} fusion(bf16[4096,256]{1,0:T(8,128)(2,1)} %all-gather.9.cloned.1.call-done, bf16[256,768]{1,0:T(8,128)(2,1)} %all-reduce.9.cloned.1.call-done), kind=kOutput, calls=%fused_computation.6 | convolution fusion | flops 1610612736 | bytes 15073280 | tf_op jit(solution)/shard_map/dot_general | solution.py:26
  218.6 4.6 %copy-done.2 = f32[4096,768]{1,0:T(8,128)} copy-done((f32[4096,768]{1,0:T(8,128)}, f32[4096,768]{1,0:T(8,128)S(1)}, u32[]{:S(2)}) %copy-start.2) | copy-done | bytes 12582936
  223.2 0.1 fusion.2
  223.3 1.6 convert_select_fusion
  225.0 59.6 %all-reduce.11.cloned.1.call-done = bf16[256,768]{1,0:T(8,128)(2,1)} async-done(((bf16[256,768]{1,0:T(8,128)(2,1)}), bf16[256,768]{1,0:T(8,128)(2,1)}) %all-reduce.11.cloned.1.call-update) | async-done | bytes 393232 | tf_op jit(solution)/shard_map/psum | solution.py:9
  284.6 7.9 %convolution_bitcast_fusion = f32[4096,768]{1,0:T(8,128)} fusion(bf16[4096,256]{1,0:T(8,128)(2,1)} %all-gather.11.cloned.1.call-done, bf16[256,768]{1,0:T(8,128)(2,1)} %all-reduce.11.cloned.1.call-done), kind=kOutput, calls=%fused_computation.5 | convolution fusion | flops 1610612736 | bytes 15073280 | tf_op jit(solution)/shard_map/dot_general | solution.py:26
  292.5 24.0 %slice_subtract_fusion = f32[3840,768]{1,0:T(8,128)} fusion(f32[4096,768]{1,0:T(8,128)} %convolution_bitcast_fusion, f32[4096,768]{1,0:T(8,128)} %copy-done.2, f32[4096,768]{1,0:T(8,128)} %copy-done.1, f32[4096,768]{1,0:T(8,128)} %copy-done, f32[4096,768]{1,0:T(8,128)} %convert_element_type.15), kind=kLoop, calls=%fused_computation.1 | loop fusion | flops 11796480 | bytes 70778880 | tf_op jit(solution)/shard_map/sub | solution.py:33
  316.5 1.3 fusion.3
  317.7 9.9 %pad_maximum_fusion = f32[4096,768]{1,0:T(8,128)} fusion(f32[3840,768]{1,0:T(8,128)} %slice_subtract_fusion, f32[256,768]{1,0:T(8,128)S(1)} %fusion.3), kind=kLoop, calls=%fused_computation | loop fusion | flops 3145728 | bytes 25165824 | tf_op jit(solution)/shard_map/concatenate | solution.py:33
  (16 shorter events, 0.2 us)
Async XLA Ops:
  7.4 66.7 %all-reduce.5.cloned.1.call-start = ((), (), s32[]{:S(2)}) async-start(), calls=%async_computation | async-start | bytes 786432 | tf_op jit(solution)/shard_map/psum | solution.py:9
  9.7 64.4 %all-gather.5.cloned.1.call-start = ((), (), s32[]{:S(2)}) async-start(), calls=%async_computation.1 | async-start | bytes 2228224 | tf_op jit(solution)/shard_map/all_gather | solution.py:27
  11.7 94.7 %all-gather.7.cloned.1.call-start = ((), (), s32[]{:S(2)}) async-start(), calls=%async_computation.3 | async-start | bytes 2228224 | tf_op jit(solution)/shard_map/all_gather | solution.py:27
  12.3 132.8 %all-reduce.7.cloned.1.call-start = ((), (), s32[]{:S(2)}) async-start(), calls=%async_computation.2 | async-start | bytes 786432 | tf_op jit(solution)/shard_map/psum | solution.py:9
  20.9 62.4 %copy-start.3 = (f32[4,256,256]{2,1,0:T(8,128)S(1)}, f32[4,256,256]{2,1,0:T(8,128)}, u32[]{:S(2)}) copy-start(f32[4,256,256]{2,1,0:T(8,128)} %param.5) | copy-start | bytes 3145732
  77.5 4.5 %copy-start = (f32[4096,768]{1,0:T(8,128)}, f32[4096,768]{1,0:T(8,128)S(1)}, u32[]{:S(2)}) copy-start(f32[4096,768]{1,0:T(8,128)S(1)} %convolution_bitcast_fusion.3) | copy-start | bytes 37748740
  85.0 70.8 %all-gather.9.cloned.1.call-start = ((), (), s32[]{:S(2)}) async-start(), calls=%async_computation.5 | async-start | bytes 2228224 | tf_op jit(solution)/shard_map/all_gather | solution.py:27
  85.6 129.6 %all-reduce.9.cloned.1.call-start = ((), (), s32[]{:S(2)}) async-start(), calls=%async_computation.4 | async-start | bytes 786432 | tf_op jit(solution)/shard_map/psum | solution.py:9
  148.5 4.5 %copy-start.1 = (f32[4096,768]{1,0:T(8,128)}, f32[4096,768]{1,0:T(8,128)S(1)}, u32[]{:S(2)}) copy-start(f32[4096,768]{1,0:T(8,128)S(1)} %convolution_bitcast_fusion.2) | copy-start | bytes 37748740
  154.8 70.2 %all-gather.11.cloned.1.call-start = ((), (), s32[]{:S(2)}) async-start(), calls=%async_computation.7 | async-start | bytes 2228224 | tf_op jit(solution)/shard_map/all_gather | solution.py:27
  155.5 129.1 %all-reduce.11.cloned.1.call-start = ((), (), s32[]{:S(2)}) async-start(), calls=%async_computation.6 | async-start | bytes 786432 | tf_op jit(solution)/shard_map/psum | solution.py:9
  218.6 4.6 %copy-start.2 = (f32[4096,768]{1,0:T(8,128)}, f32[4096,768]{1,0:T(8,128)S(1)}, u32[]{:S(2)}) copy-start(f32[4096,768]{1,0:T(8,128)S(1)} %convolution_bitcast_fusion.1) | copy-start | bytes 37748740
Sparse Core Ops, SparseCore 0:
  10.5 63.5 all-reduce.4
  85.1 59.8 all-reduce.6
  154.9 60.2 all-reduce.8
  225.1 59.4 all-reduce.10
Sparse Core Ops, SparseCore 1:
  12.3 47.6 all-gather.4
  62.0 44.3 all-gather.6
  108.4 44.3 all-gather.8
  157.7 44.2 all-gather.10
where the time goes:
time: 335 us
  waiting for transfers between devices  233 us (70%)
  other arithmetic  45.3 us (14%)
  matrix products  25.3 us (8%)
  local copies, waits for them, and re-layouts  15.5 us (5%)
  between operations  15 us (4%)
    psum x4, waiting for transfers between devices, from_root(): return lax.psum(jnp.where(mine, value, jnp.zeros_like(value)), axis)  211 us
    sub x1, other arithmetic, per_device(): current[panel_width:] - update[panel_width:]  24 us
    all_gather x4, waiting for transfers between devices, per_device(): lax.all_gather(columns, 'col', axis=0, tiled=True)  20.8 us
    dot_general x4, matrix products, per_device(): jnp.dot(lax.all_gather(columns, 'col', axis=0, tiled=True), shared, prefe...  18.2 us
    unnamed x8, local copies, waits for them, and re-layouts  13.6 us
    concatenate x1, other arithmetic, per_device(): jnp.concatenate([new_first, current[panel_width:] - update[panel_width:]]...  9.94 us
    convert_element_type x1, other arithmetic, per_device(): current = right_sides.astype(jnp.float32)  8.55 us
    dot_general x4, matrix products, per_device(): jnp.dot(inverse_blocks[panel_num], leading, precision=lax.Precision.HIGHEST)  7.15 us
  transfers between devices with their start and end apart: 8, of which 5 were waited for; matrix products, arithmetic and copies ran while one was open for 8% of the time, Pallas kernels for 0%

commit v1 on v0

--- a/solution.py
+++ b/solution.py
@@ -23,10 +23,35 @@
         solved = jnp.dot(inverse_blocks[panel_num], leading, precision=lax.Precision.HIGHEST)
         shared = publish(solved, panel_num)
         columns = factor_panels[:, panel_num * panel_width : (panel_num + 1) * panel_width]
+
+        def _convert_sums_all(z, ax_name):
+            lower = lax.axis_index(ax_name)
+            upper = lax.axis_size(ax_name)
+            response, r_now, z1 = (upper, lower, z.shape[0])
+            kept_rows = [b * response if m == 0 else b for m, b in enumerate(z.shape)]
+            parts_out = jnp.zeros(kept_rows, z.dtype)
+            x_new = block_now = z
+            dev = 1
+            current_value = lax.dynamic_update_slice_in_dim(parts_out, z, r_now * z1, axis=0)
+            while dev < response // 2 + 1:
+                x_new = lax.ppermute(
+                    x_new, ax_name, [(m, (m + 1) % response) for m in range(response)]
+                )
+                current_value = lax.dynamic_update_slice_in_dim(
+                    current_value, x_new, (r_now - dev) % response * z1, axis=0
+                )
+                if 2 * dev < response:
+                    block_now = lax.ppermute(
+                        block_now, ax_name, [(m, (m - 1) % response) for m in range(response)]
+                    )
+                    current_value = lax.dynamic_update_slice_in_dim(
+                        current_value, block_now, (r_now + dev) % response * z1, axis=0
+                    )
+                dev += 1
+            return current_value
+
         update = jnp.dot(
-            lax.all_gather(columns, "col", axis=0, tiled=True),
-            shared,
-            preferred_element_type=jnp.float32,
+            _convert_sums_all(columns, "col"), shared, preferred_element_type=jnp.float32
         )
         updated_first = jnp.where(row_index > panel_num, leading - update[:panel_width], leading)
         new_first = jnp.where(row_index == panel_num, solved, updated_first)

time: 335 us -> 489 us (1.46); the launches traced: 335 us -> 480 us
  starting transfers between devices: 0.48 us -> 151 us
  waiting for transfers between devices: 233 us -> 187 us
  local copies, waits for them, and re-layouts: 15.5 us -> 55 us
    ppermute x0 -> x60, starting transfers between devices: none -> 151 us  [the longest x28 149 us: _convert_sums_all(): lax.ppermute(block_now, ax_name, [(m, (m - 1) % response) for m in range(...]
    dynamic_update_slice x0 -> x63, local copies, waits for them, and re-layouts: none -> 37 us  [the longest x32 20.7 us: _convert_sums_all(): lax.dynamic_update_slice_in_dim(current_value, x_new, (r_now - dev) % res...]
    psum x4, waiting for transfers between devices: 211 us -> 175 us  [from_root(): return lax.psum(jnp.where(mine, value, jnp.zeros_like(value)), axis)]
    all_gather x4 -> x0, waiting for transfers between devices: 20.8 us -> none  [per_device(): lax.all_gather(columns, 'col', axis=0, tiled=True)]
    ppermute x0 -> x60, waiting for transfers between devices: none -> 11.8 us  [the longest x32 11.7 us: _convert_sums_all(): lax.ppermute(x_new, ax_name, [(m, (m + 1) % response) for m in range(resp...]
    unnamed x8 -> x16, local copies, waits for them, and re-layouts: 13.6 us -> 14.6 us
  transfers between devices with their start and end apart: 8 -> 64, of which waited for: 5 -> 6; matrix products, arithmetic and copies ran while one was open for 8% -> 15% of each run, Pallas kernels for 0% -> 0%
where the time goes in v1:
time: 489 us; the launch traced here: 480 us
  waiting for transfers between devices  187 us (38%)
  starting transfers between devices  151 us (31%)
  local copies, waits for them, and re-layouts  55 us (11%)
  other arithmetic  45.4 us (9%)
  matrix products  27.8 us (6%)
  between operations  13.8 us (3%)
    psum x4, waiting for transfers between devices, from_root(): return lax.psum(jnp.where(mine, value, jnp.zeros_like(value)), axis)  175 us
    ppermute x28, starting transfers between devices, _convert_sums_all(): lax.ppermute(block_now, ax_name, [(m, (m - 1) % response) for m in range(...  149 us
    sub x1, other arithmetic, per_device(): current[panel_width:] - update[panel_width:]  24 us
    dynamic_update_slice x32, local copies, waits for them, and re-layouts, _convert_sums_all(): lax.dynamic_update_slice_in_dim(current_value, x_new, (r_now - dev) % res...  20.7 us
    dot_general x4, matrix products, per_device(): jnp.dot(_convert_sums_all(columns, 'col'), shared, preferred_element_type...  17.1 us
    dynamic_update_slice x28, local copies, waits for them, and re-layouts, _convert_sums_all(): lax.dynamic_update_slice_in_dim(current_value, block_now, (r_now + dev) %...  15 us
    unnamed x16, local copies, waits for them, and re-layouts  14.6 us
    ppermute x32, waiting for transfers between devices, _convert_sums_all(): lax.ppermute(x_new, ax_name, [(m, (m + 1) % response) for m in range(resp...  11.7 us
  transfers between devices with their start and end apart: 64, of which 6 were waited for; matrix products, arithmetic and copies ran while one was open for 15% of the time, Pallas kernels for 0%

profile of v1, /device:TPU:0, one launch (start us, length us, event | category | flops | bytes accessed | tf_op | source)
XLA Modules:
  0.0 479.6 jit_solution(5531491535178529010)
XLA Ops:
  14.4 5.3 %collective-permute-start.1 = (bf16[256,256]{1,0:T(8,128)(2,1)S(1)}, bf16[256,256]{1,0:T(8,128)(2,1)S(1)}, u32[]{:S(2)}, u32[]{:S(2)}) collective-permute-start(bf16[256,256]{1,0:T(8,128)(2,1)S(1)} %get-tuple-element.8), channel_id=1, source_target_pairs={{0,15},{1,0},{2,1},{3,2},{4,3},{5,4},{6,5},{7,6},{8,7},{9,8},{10,9... | collective-permute-start | bytes 393224 | tf_op jit(solution)/shard_map/ppermute | solution.py:44
  27.0 8.6 %convert_element_type.15 = f32[4096,768]{1,0:T(8,128)} convert(bf16[4096,768]{1,0:T(8,128)(2,1)} %param.3) | non-fusion elementwise | flops 3145728 | bytes 18874368 | tf_op jit(solution)/shard_map/convert_element_type | solution.py:20
  42.4 5.4 %collective-permute-start.46 = (bf16[256,256]{1,0:T(8,128)(2,1)S(1)}, bf16[256,256]{1,0:T(8,128)(2,1)S(1)}, u32[]{:S(2)}, u32[]{:S(2)}) collective-permute-start(bf16[256,256]{1,0:T(8,128)(2,1)S(1)} %get-tuple-element.9), channel_id=1, source_target_pairs={{0,15},{1,0},{2,1},{3,2},{4,3},{5,4},{6,5},{7,6},{8,7},{9,8},{10,9... | collective-permute-start | bytes 393224 | tf_op jit(solution)/shard_map/ppermute | solution.py:44
  48.5 5.4 %collective-permute-start.18 = (bf16[256,256]{1,0:T(8,128)(2,1)S(1)}, bf16[256,256]{1,0:T(8,128)(2,1)S(1)}, u32[]{:S(2)}, u32[]{:S(2)}) collective-permute-start(bf16[256,256]{1,0:T(8,128)(2,1)S(1)} %collective-permute-done.16), channel_id=1, source_target_pairs={{0,15},{1,0},{2,1},{3,2},{4,3},{5,4},{6,5},{7,6},{8,7},{9,8},{10,9... | collective-permute-start | bytes 393224 | tf_op jit(solution)/shard_map/ppermute | solution.py:44
  56.2 5.3 %collective-permute-start.3 = (bf16[256,256]{1,0:T(8,128)(2,1)S(1)}, bf16[256,256]{1,0:T(8,128)(2,1)S(1)}, u32[]{:S(2)}, u32[]{:S(2)}) collective-permute-start(bf16[256,256]{1,0:T(8,128)(2,1)S(1)} %collective-permute-done.1), channel_id=1, source_target_pairs={{0,15},{1,0},{2,1},{3,2},{4,3},{5,4},{6,5},{7,6},{8,7},{9,8},{10,9... | collective-permute-start | bytes 393224 | tf_op jit(solution)/shard_map/ppermute | solution.py:44
  68.9 5.4 %collective-permute-start.48 = (bf16[256,256]{1,0:T(8,128)(2,1)S(1)}, bf16[256,256]{1,0:T(8,128)(2,1)S(1)}, u32[]{:S(2)}, u32[]{:S(2)}) collective-permute-start(bf16[256,256]{1,0:T(8,128)(2,1)S(1)} %collective-permute-done.46), channel_id=1, source_target_pairs={{0,15},{1,0},{2,1},{3,2},{4,3},{5,4},{6,5},{7,6},{8,7},{9,8},{10,9... | collective-permute-start | bytes 393224 | tf_op jit(solution)/shard_map/ppermute | solution.py:44
  74.9 5.4 %collective-permute-start.20 = (bf16[256,256]{1,0:T(8,128)(2,1)S(1)}, bf16[256,256]{1,0:T(8,128)(2,1)S(1)}, u32[]{:S(2)}, u32[]{:S(2)}) collective-permute-start(bf16[256,256]{1,0:T(8,128)(2,1)S(1)} %collective-permute-done.18), channel_id=1, source_target_pairs={{0,15},{1,0},{2,1},{3,2},{4,3},{5,4},{6,5},{7,6},{8,7},{9,8},{10,9... | collective-permute-start | bytes 393224 | tf_op jit(solution)/shard_map/ppermute | solution.py:44
  81.7 5.3 %collective-permute-start.5 = (bf16[256,256]{1,0:T(8,128)(2,1)S(1)}, bf16[256,256]{1,0:T(8,128)(2,1)S(1)}, u32[]{:S(2)}, u32[]{:S(2)}) collective-permute-start(bf16[256,256]{1,0:T(8,128)(2,1)S(1)} %collective-permute-done.3), channel_id=1, source_target_pairs={{0,15},{1,0},{2,1},{3,2},{4,3},{5,4},{6,5},{7,6},{8,7},{9,8},{10,9... | collective-permute-start | bytes 393224 | tf_op jit(solution)/shard_map/ppermute | solution.py:44
  88.3 5.4 %collective-permute-start.35 = (bf16[256,256]{1,0:T(8,128)(2,1)S(1)}, bf16[256,256]{1,0:T(8,128)(2,1)S(1)}, u32[]{:S(2)}, u32[]{:S(2)}) collective-permute-start(bf16[256,256]{1,0:T(8,128)(2,1)S(1)} %collective-permute-done.33), channel_id=1, source_target_pairs={{0,15},{1,0},{2,1},{3,2},{4,3},{5,4},{6,5},{7,6},{8,7},{9,8},{10,9... | collective-permute-start | bytes 393224 | tf_op jit(solution)/shard_map/ppermute | solution.py:44
  94.4 5.9 %collective-permute-start.50 = (bf16[256,256]{1,0:T(8,128)(2,1)S(1)}, bf16[256,256]{1,0:T(8,128)(2,1)S(1)}, u32[]{:S(2)}, u32[]{:S(2)}) collective-permute-start(bf16[256,256]{1,0:T(8,128)(2,1)S(1)} %collective-permute-done.48), channel_id=1, source_target_pairs={{0,15},{1,0},{2,1},{3,2},{4,3},{5,4},{6,5},{7,6},{8,7},{9,8},{10,9... | collective-permute-start | bytes 393224 | tf_op jit(solution)/shard_map/ppermute | solution.py:44
  101.0 5.4 %collective-permute-start.22 = (bf16[256,256]{1,0:T(8,128)(2,1)S(1)}, bf16[256,256]{1,0:T(8,128)(2,1)S(1)}, u32[]{:S(2)}, u32[]{:S(2)}) collective-permute-start(bf16[256,256]{1,0:T(8,128)(2,1)S(1)} %collective-permute-done.20), channel_id=1, source_target_pairs={{0,15},{1,0},{2,1},{3,2},{4,3},{5,4},{6,5},{7,6},{8,7},{9,8},{10,9... | collective-permute-start | bytes 393224 | tf_op jit(solution)/shard_map/ppermute | solution.py:44
  107.7 5.3 %collective-permute-start.7 = (bf16[256,256]{1,0:T(8,128)(2,1)S(1)}, bf16[256,256]{1,0:T(8,128)(2,1)S(1)}, u32[]{:S(2)}, u32[]{:S(2)}) collective-permute-start(bf16[256,256]{1,0:T(8,128)(2,1)S(1)} %collective-permute-done.5), channel_id=1, source_target_pairs={{0,15},{1,0},{2,1},{3,2},{4,3},{5,4},{6,5},{7,6},{8,7},{9,8},{10,9... | collective-permute-start | bytes 393224 | tf_op jit(solution)/shard_map/ppermute | solution.py:44
  114.4 5.3 %collective-permute-start.37 = (bf16[256,256]{1,0:T(8,128)(2,1)S(1)}, bf16[256,256]{1,0:T(8,128)(2,1)S(1)}, u32[]{:S(2)}, u32[]{:S(2)}) collective-permute-start(bf16[256,256]{1,0:T(8,128)(2,1)S(1)} %collective-permute-done.35), channel_id=1, source_target_pairs={{0,15},{1,0},{2,1},{3,2},{4,3},{5,4},{6,5},{7,6},{8,7},{9,8},{10,9... | collective-permute-start | bytes 393224 | tf_op jit(solution)/shard_map/ppermute | solution.py:44
  120.4 5.4 %collective-permute-start.52 = (bf16[256,256]{1,0:T(8,128)(2,1)S(1)}, bf16[256,256]{1,0:T(8,128)(2,1)S(1)}, u32[]{:S(2)}, u32[]{:S(2)}) collective-permute-start(bf16[256,256]{1,0:T(8,128)(2,1)S(1)} %collective-permute-done.50), channel_id=1, source_target_pairs={{0,15},{1,0},{2,1},{3,2},{4,3},{5,4},{6,5},{7,6},{8,7},{9,8},{10,9... | collective-permute-start | bytes 393224 | tf_op jit(solution)/shard_map/ppermute | solution.py:44
  126.5 5.4 %collective-permute-start.24 = (bf16[256,256]{1,0:T(8,128)(2,1)S(1)}, bf16[256,256]{1,0:T(8,128)(2,1)S(1)}, u32[]{:S(2)}, u32[]{:S(2)}) collective-permute-start(bf16[256,256]{1,0:T(8,128)(2,1)S(1)} %collective-permute-done.22), channel_id=1, source_target_pairs={{0,15},{1,0},{2,1},{3,2},{4,3},{5,4},{6,5},{7,6},{8,7},{9,8},{10,9... | collective-permute-start | bytes 393224 | tf_op jit(solution)/shard_map/ppermute | solution.py:44
  133.2 5.3 %collective-permute-start.9 = (bf16[256,256]{1,0:T(8,128)(2,1)S(1)}, bf16[256,256]{1,0:T(8,128)(2,1)S(1)}, u32[]{:S(2)}, u32[]{:S(2)}) collective-permute-start(bf16[256,256]{1,0:T(8,128)(2,1)S(1)} %collective-permute-done.7), channel_id=1, source_target_pairs={{0,15},{1,0},{2,1},{3,2},{4,3},{5,4},{6,5},{7,6},{8,7},{9,8},{10,9... | collective-permute-start | bytes 393224 | tf_op jit(solution)/shard_map/ppermute | solution.py:44
  139.9 5.4 %collective-permute-start.39 = (bf16[256,256]{1,0:T(8,128)(2,1)S(1)}, bf16[256,256]{1,0:T(8,128)(2,1)S(1)}, u32[]{:S(2)}, u32[]{:S(2)}) collective-permute-start(bf16[256,256]{1,0:T(8,128)(2,1)S(1)} %collective-permute-done.37), channel_id=1, source_target_pairs={{0,15},{1,0},{2,1},{3,2},{4,3},{5,4},{6,5},{7,6},{8,7},{9,8},{10,9... | collective-permute-start | bytes 393224 | tf_op jit(solution)/shard_map/ppermute | solution.py:44
  145.9 5.4 %collective-permute-start.54 = (bf16[256,256]{1,0:T(8,128)(2,1)S(1)}, bf16[256,256]{1,0:T(8,128)(2,1)S(1)}, u32[]{:S(2)}, u32[]{:S(2)}) collective-permute-start(bf16[256,256]{1,0:T(8,128)(2,1)S(1)} %collective-permute-done.52), channel_id=1, source_target_pairs={{0,15},{1,0},{2,1},{3,2},{4,3},{5,4},{6,5},{7,6},{8,7},{9,8},{10,9... | collective-permute-start | bytes 393224 | tf_op jit(solution)/shard_map/ppermute | solution.py:44
  152.0 5.4 %collective-permute-start.26 = (bf16[256,256]{1,0:T(8,128)(2,1)S(1)}, bf16[256,256]{1,0:T(8,128)(2,1)S(1)}, u32[]{:S(2)}, u32[]{:S(2)}) collective-permute-start(bf16[256,256]{1,0:T(8,128)(2,1)S(1)} %collective-permute-done.24), channel_id=1, source_target_pairs={{0,15},{1,0},{2,1},{3,2},{4,3},{5,4},{6,5},{7,6},{8,7},{9,8},{10,9... | collective-permute-start | bytes 393224 | tf_op jit(solution)/shard_map/ppermute | solution.py:44
  158.8 5.3 %collective-permute-start.11 = (bf16[256,256]{1,0:T(8,128)(2,1)S(1)}, bf16[256,256]{1,0:T(8,128)(2,1)S(1)}, u32[]{:S(2)}, u32[]{:S(2)}) collective-permute-start(bf16[256,256]{1,0:T(8,128)(2,1)S(1)} %collective-permute-done.9), channel_id=1, source_target_pairs={{0,15},{1,0},{2,1},{3,2},{4,3},{5,4},{6,5},{7,6},{8,7},{9,8},{10,9... | collective-permute-start | bytes 393224 | tf_op jit(solution)/shard_map/ppermute | solution.py:44
  165.4 5.3 %collective-permute-start.41 = (bf16[256,256]{1,0:T(8,128)(2,1)S(1)}, bf16[256,256]{1,0:T(8,128)(2,1)S(1)}, u32[]{:S(2)}, u32[]{:S(2)}) collective-permute-start(bf16[256,256]{1,0:T(8,128)(2,1)S(1)} %collective-permute-done.39), channel_id=1, source_target_pairs={{0,15},{1,0},{2,1},{3,2},{4,3},{5,4},{6,5},{7,6},{8,7},{9,8},{10,9... | collective-permute-start | bytes 393224 | tf_op jit(solution)/shard_map/ppermute | solution.py:44
  171.5 5.4 %collective-permute-start.56 = (bf16[256,256]{1,0:T(8,128)(2,1)S(1)}, bf16[256,256]{1,0:T(8,128)(2,1)S(1)}, u32[]{:S(2)}, u32[]{:S(2)}) collective-permute-start(bf16[256,256]{1,0:T(8,128)(2,1)S(1)} %collective-permute-done.54), channel_id=1, source_target_pairs={{0,15},{1,0},{2,1},{3,2},{4,3},{5,4},{6,5},{7,6},{8,7},{9,8},{10,9... | collective-permute-start | bytes 393224 | tf_op jit(solution)/shard_map/ppermute | solution.py:44
  177.6 5.4 %collective-permute-start.28 = (bf16[256,256]{1,0:T(8,128)(2,1)S(1)}, bf16[256,256]{1,0:T(8,128)(2,1)}, u32[]{:S(2)}, u32[]{:S(2)}) collective-permute-start(bf16[256,256]{1,0:T(8,128)(2,1)S(1)} %collective-permute-done.26), channel_id=1, source_target_pairs={{0,15},{1,0},{2,1},{3,2},{4,3},{5,4},{6,5},{7,6},{8,7},{9,8},{10,9... | collective-permute-start | bytes 393224 | tf_op jit(solution)/shard_map/ppermute | solution.py:44
  184.3 5.4 %collective-permute-start.13 = (bf16[256,256]{1,0:T(8,128)(2,1)S(1)}, bf16[256,256]{1,0:T(8,128)(2,1)S(1)}, u32[]{:S(2)}, u32[]{:S(2)}) collective-permute-start(bf16[256,256]{1,0:T(8,128)(2,1)S(1)} %collective-permute-done.11), channel_id=1, source_target_pairs={{0,15},{1,0},{2,1},{3,2},{4,3},{5,4},{6,5},{7,6},{8,7},{9,8},{10,9... | collective-permute-start | bytes 393224 | tf_op jit(solution)/shard_map/ppermute | solution.py:44
  191.0 5.3 %collective-permute-start.43 = (bf16[256,256]{1,0:T(8,128)(2,1)S(1)}, bf16[256,256]{1,0:T(8,128)(2,1)}, u32[]{:S(2)}, u32[]{:S(2)}) collective-permute-start(bf16[256,256]{1,0:T(8,128)(2,1)S(1)} %collective-permute-done.41), channel_id=1, source_target_pairs={{0,15},{1,0},{2,1},{3,2},{4,3},{5,4},{6,5},{7,6},{8,7},{9,8},{10,9... | collective-permute-start | bytes 393224 | tf_op jit(solution)/shard_map/ppermute | solution.py:44
  207.7 7.6 %collective-permute-done.14 = bf16[256,256]{1,0:T(8,128)(2,1)S(1)} collective-permute-done((bf16[256,256]{1,0:T(8,128)(2,1)S(1)}, bf16[256,256]{1,0:T(8,128)(2,1)S(1)}, u32[]{:S(2)}, u32[]{:S(2)}) %collective-permute-start.14) | collective-permute-done | bytes 131104 | tf_op jit(solution)/shard_map/ppermute | solution.py:37
  229.1 59.8 %all-reduce.7.cloned.1.call-done = bf16[256,768]{1,0:T(8,128)(2,1)} async-done(((bf16[256,768]{1,0:T(8,128)(2,1)}), bf16[256,768]{1,0:T(8,128)(2,1)}) %all-reduce.7.cloned.1.call-update) | async-done | bytes 393232 | tf_op jit(solution)/shard_map/psum | solution.py:9
  302.5 56.5 %all-reduce.9.cloned.1.call-done = bf16[256,768]{1,0:T(8,128)(2,1)} async-done(((bf16[256,768]{1,0:T(8,128)(2,1)}), bf16[256,768]{1,0:T(8,128)(2,1)}) %all-reduce.9.cloned.1.call-update) | async-done | bytes 393232 | tf_op jit(solution)/shard_map/psum | solution.py:9
  371.1 58.6 %all-reduce.11.cloned.1.call-done = bf16[256,768]{1,0:T(8,128)(2,1)} async-done(((bf16[256,768]{1,0:T(8,128)(2,1)}), bf16[256,768]{1,0:T(8,128)(2,1)}) %all-reduce.11.cloned.1.call-update) | async-done | bytes 393232 | tf_op jit(solution)/shard_map/psum | solution.py:9
  429.7 8.0 %fusion.18 = f32[4096,768]{1,0:T(8,128)} fusion(bf16[4096,256]{1,0:T(8,128)(2,1)} %constant_dynamic-update-slice_fusion, bf16[256,768]{1,0:T(8,128)(2,1)} %all-reduce.11.cloned.1.call-done), kind=kOutput, calls=%fused_computation.98 | convolution fusion | flops 1610612736 | bytes 15073280 | tf_op jit(solution)/shard_map/dot_general | solution.py:53
  437.7 24.0 %slice_subtract_fusion = f32[3840,768]{1,0:T(8,128)} fusion(f32[4096,768]{1,0:T(8,128)} %fusion.18, f32[4096,768]{1,0:T(8,128)} %copy-done.2, f32[4096,768]{1,0:T(8,128)} %copy-done.1, f32[4096,768]{1,0:T(8,128)} %copy-done, f32[4096,768]{1,0:T(8,128)} %convert_element_type.15), kind=kLoop, calls=%fused_computation.1 | loop fusion | flops 11796480 | bytes 70778880 | tf_op jit(solution)/shard_map/sub | solution.py:58
  462.9 9.9 %pad_maximum_fusion = f32[4096,768]{1,0:T(8,128)} fusion(f32[3840,768]{1,0:T(8,128)} %slice_subtract_fusion, f32[256,768]{1,0:T(8,128)S(1)} %fusion.3), kind=kLoop, calls=%fused_computation | loop fusion | flops 3145728 | bytes 25165824 | tf_op jit(solution)/shard_map/concatenate | solution.py:58
  (199 shorter events, 103.4 us)
Async XLA Ops:
  6.5 208.8 %all-reduce.5.cloned.1.call-start = ((), (), s32[]{:S(2)}) async-start(), calls=%async_computation | async-start | bytes 786432 | tf_op jit(solution)/shard_map/psum | solution.py:9
  7.6 27.9 %collective-permute-start.15 = (bf16[256,256]{1,0:T(8,128)(2,1)S(1)}, bf16[256,256]{1,0:T(8,128)(2,1)}, u32[]{:S(2)}, u32[]{:S(2)}) collective-permute-start(bf16[256,256]{1,0:T(8,128)(2,1)S(1)} %get-tuple-element.7), channel_id=1, source_target_pairs={{0,1},{1,2},{2,3},{3,4},{4,5},{5,6},{6,7},{7,8},{8,9},{9,10},{10,1... | collective-permute-start | bytes 393224 | tf_op jit(solution)/shard_map/ppermute | solution.py:37
  9.4 33.0 %collective-permute-start.16 = (bf16[256,256]{1,0:T(8,128)(2,1)S(1)}, bf16[256,256]{1,0:T(8,128)(2,1)S(1)}, u32[]{:S(2)}, u32[]{:S(2)}) collective-permute-start(bf16[256,256]{1,0:T(8,128)(2,1)S(1)} %get-tuple-element.7), channel_id=1, source_target_pairs={{0,15},{1,0},{2,1},{3,2},{4,3},{5,4},{6,5},{7,6},{8,7},{9,8},{10,9... | collective-permute-start | bytes 393224 | tf_op jit(solution)/shard_map/ppermute | solution.py:44
  14.4 28.0 %collective-permute-start = (bf16[256,256]{1,0:T(8,128)(2,1)S(1)}, bf16[256,256]{1,0:T(8,128)(2,1)S(1)}, u32[]{:S(2)}, u32[]{:S(2)}) collective-permute-start(bf16[256,256]{1,0:T(8,128)(2,1)S(1)} %get-tuple-element.8), channel_id=1, source_target_pairs={{0,1},{1,2},{2,3},{3,4},{4,5},{5,6},{6,7},{7,8},{8,9},{9,10},{10,1... | collective-permute-start | bytes 393224 | tf_op jit(solution)/shard_map/ppermute | solution.py:37
  14.4 34.1 %collective-permute-start.1 = (bf16[256,256]{1,0:T(8,128)(2,1)S(1)}, bf16[256,256]{1,0:T(8,128)(2,1)S(1)}, u32[]{:S(2)}, u32[]{:S(2)}) collective-permute-start(bf16[256,256]{1,0:T(8,128)(2,1)S(1)} %get-tuple-element.8), channel_id=1, source_target_pairs={{0,15},{1,0},{2,1},{3,2},{4,3},{5,4},{6,5},{7,6},{8,7},{9,8},{10,9... | collective-permute-start | bytes 393224 | tf_op jit(solution)/shard_map/ppermute | solution.py:44
  22.3 266.6 %all-reduce.7.cloned.1.call-start = ((), (), s32[]{:S(2)}) async-start(), calls=%async_computation.1 | async-start | bytes 786432 | tf_op jit(solution)/shard_map/psum | solution.py:9
  22.4 26.1 %collective-permute-start.30 = (bf16[256,256]{1,0:T(8,128)(2,1)S(1)}, bf16[256,256]{1,0:T(8,128)(2,1)}, u32[]{:S(2)}, u32[]{:S(2)}) collective-permute-start(bf16[256,256]{1,0:T(8,128)(2,1)S(1)} %get-tuple-element.5), channel_id=1, source_target_pairs={{0,1},{1,2},{2,3},{3,4},{4,5},{5,6},{6,7},{7,8},{8,9},{9,10},{10,1... | collective-permute-start | bytes 393224 | tf_op jit(solution)/shard_map/ppermute | solution.py:37
  35.5 20.0 %collective-permute-start.31 = (bf16[256,256]{1,0:T(8,128)(2,1)S(1)}, bf16[256,256]{1,0:T(8,128)(2,1)S(1)}, u32[]{:S(2)}, u32[]{:S(2)}) collective-permute-start(bf16[256,256]{1,0:T(8,128)(2,1)S(1)} %get-tuple-element.5), channel_id=1, source_target_pairs={{0,15},{1,0},{2,1},{3,2},{4,3},{5,4},{6,5},{7,6},{8,7},{9,8},{10,9... | collective-permute-start | bytes 393224 | tf_op jit(solution)/shard_map/ppermute | solution.py:44
  42.4 19.7 %collective-permute-start.46 = (bf16[256,256]{1,0:T(8,128)(2,1)S(1)}, bf16[256,256]{1,0:T(8,128)(2,1)S(1)}, u32[]{:S(2)}, u32[]{:S(2)}) collective-permute-start(bf16[256,256]{1,0:T(8,128)(2,1)S(1)} %get-tuple-element.9), channel_id=1, source_target_pairs={{0,15},{1,0},{2,1},{3,2},{4,3},{5,4},{6,5},{7,6},{8,7},{9,8},{10,9... | collective-permute-start | bytes 393224 | tf_op jit(solution)/shard_map/ppermute | solution.py:44
  48.5 20.3 %collective-permute-start.18 = (bf16[256,256]{1,0:T(8,128)(2,1)S(1)}, bf16[256,256]{1,0:T(8,128)(2,1)S(1)}, u32[]{:S(2)}, u32[]{:S(2)}) collective-permute-start(bf16[256,256]{1,0:T(8,128)(2,1)S(1)} %collective-permute-done.16), channel_id=1, source_target_pairs={{0,15},{1,0},{2,1},{3,2},{4,3},{5,4},{6,5},{7,6},{8,7},{9,8},{10,9... | collective-permute-start | bytes 393224 | tf_op jit(solution)/shard_map/ppermute | solution.py:44
  68.9 18.8 %collective-permute-start.48 = (bf16[256,256]{1,0:T(8,128)(2,1)S(1)}, bf16[256,256]{1,0:T(8,128)(2,1)S(1)}, u32[]{:S(2)}, u32[]{:S(2)}) collective-permute-start(bf16[256,256]{1,0:T(8,128)(2,1)S(1)} %collective-permute-done.46), channel_id=1, source_target_pairs={{0,15},{1,0},{2,1},{3,2},{4,3},{5,4},{6,5},{7,6},{8,7},{9,8},{10,9... | collective-permute-start | bytes 393224 | tf_op jit(solution)/shard_map/ppermute | solution.py:44
  74.9 19.4 %collective-permute-start.20 = (bf16[256,256]{1,0:T(8,128)(2,1)S(1)}, bf16[256,256]{1,0:T(8,128)(2,1)S(1)}, u32[]{:S(2)}, u32[]{:S(2)}) collective-permute-start(bf16[256,256]{1,0:T(8,128)(2,1)S(1)} %collective-permute-done.18), channel_id=1, source_target_pairs={{0,15},{1,0},{2,1},{3,2},{4,3},{5,4},{6,5},{7,6},{8,7},{9,8},{10,9... | collective-permute-start | bytes 393224 | tf_op jit(solution)/shard_map/ppermute | solution.py:44
  81.7 19.2 %collective-permute-start.5 = (bf16[256,256]{1,0:T(8,128)(2,1)S(1)}, bf16[256,256]{1,0:T(8,128)(2,1)S(1)}, u32[]{:S(2)}, u32[]{:S(2)}) collective-permute-start(bf16[256,256]{1,0:T(8,128)(2,1)S(1)} %collective-permute-done.3), channel_id=1, source_target_pairs={{0,15},{1,0},{2,1},{3,2},{4,3},{5,4},{6,5},{7,6},{8,7},{9,8},{10,9... | collective-permute-start | bytes 393224 | tf_op jit(solution)/shard_map/ppermute | solution.py:44
  94.4 19.3 %collective-permute-start.50 = (bf16[256,256]{1,0:T(8,128)(2,1)S(1)}, bf16[256,256]{1,0:T(8,128)(2,1)S(1)}, u32[]{:S(2)}, u32[]{:S(2)}) collective-permute-start(bf16[256,256]{1,0:T(8,128)(2,1)S(1)} %collective-permute-done.48), channel_id=1, source_target_pairs={{0,15},{1,0},{2,1},{3,2},{4,3},{5,4},{6,5},{7,6},{8,7},{9,8},{10,9... | collective-permute-start | bytes 393224 | tf_op jit(solution)/shard_map/ppermute | solution.py:44
  101.0 19.4 %collective-permute-start.22 = (bf16[256,256]{1,0:T(8,128)(2,1)S(1)}, bf16[256,256]{1,0:T(8,128)(2,1)S(1)}, u32[]{:S(2)}, u32[]{:S(2)}) collective-permute-start(bf16[256,256]{1,0:T(8,128)(2,1)S(1)} %collective-permute-done.20), channel_id=1, source_target_pairs={{0,15},{1,0},{2,1},{3,2},{4,3},{5,4},{6,5},{7,6},{8,7},{9,8},{10,9... | collective-permute-start | bytes 393224 | tf_op jit(solution)/shard_map/ppermute | solution.py:44
  107.7 18.8 %collective-permute-start.7 = (bf16[256,256]{1,0:T(8,128)(2,1)S(1)}, bf16[256,256]{1,0:T(8,128)(2,1)S(1)}, u32[]{:S(2)}, u32[]{:S(2)}) collective-permute-start(bf16[256,256]{1,0:T(8,128)(2,1)S(1)} %collective-permute-done.5), channel_id=1, source_target_pairs={{0,15},{1,0},{2,1},{3,2},{4,3},{5,4},{6,5},{7,6},{8,7},{9,8},{10,9... | collective-permute-start | bytes 393224 | tf_op jit(solution)/shard_map/ppermute | solution.py:44
  120.4 18.8 %collective-permute-start.52 = (bf16[256,256]{1,0:T(8,128)(2,1)S(1)}, bf16[256,256]{1,0:T(8,128)(2,1)S(1)}, u32[]{:S(2)}, u32[]{:S(2)}) collective-permute-start(bf16[256,256]{1,0:T(8,128)(2,1)S(1)} %collective-permute-done.50), channel_id=1, source_target_pairs={{0,15},{1,0},{2,1},{3,2},{4,3},{5,4},{6,5},{7,6},{8,7},{9,8},{10,9... | collective-permute-start | bytes 393224 | tf_op jit(solution)/shard_map/ppermute | solution.py:44
  126.5 19.4 %collective-permute-start.24 = (bf16[256,256]{1,0:T(8,128)(2,1)S(1)}, bf16[256,256]{1,0:T(8,128)(2,1)S(1)}, u32[]{:S(2)}, u32[]{:S(2)}) collective-permute-start(bf16[256,256]{1,0:T(8,128)(2,1)S(1)} %collective-permute-done.22), channel_id=1, source_target_pairs={{0,15},{1,0},{2,1},{3,2},{4,3},{5,4},{6,5},{7,6},{8,7},{9,8},{10,9... | collective-permute-start | bytes 393224 | tf_op jit(solution)/shard_map/ppermute | solution.py:44
  133.2 18.8 %collective-permute-start.9 = (bf16[256,256]{1,0:T(8,128)(2,1)S(1)}, bf16[256,256]{1,0:T(8,128)(2,1)S(1)}, u32[]{:S(2)}, u32[]{:S(2)}) collective-permute-start(bf16[256,256]{1,0:T(8,128)(2,1)S(1)} %collective-permute-done.7), channel_id=1, source_target_pairs={{0,15},{1,0},{2,1},{3,2},{4,3},{5,4},{6,5},{7,6},{8,7},{9,8},{10,9... | collective-permute-start | bytes 393224 | tf_op jit(solution)/shard_map/ppermute | solution.py:44
  145.9 18.9 %collective-permute-start.54 = (bf16[256,256]{1,0:T(8,128)(2,1)S(1)}, bf16[256,256]{1,0:T(8,128)(2,1)S(1)}, u32[]{:S(2)}, u32[]{:S(2)}) collective-permute-start(bf16[256,256]{1,0:T(8,128)(2,1)S(1)} %collective-permute-done.52), channel_id=1, source_target_pairs={{0,15},{1,0},{2,1},{3,2},{4,3},{5,4},{6,5},{7,6},{8,7},{9,8},{10,9... | collective-permute-start | bytes 393224 | tf_op jit(solution)/shard_map/ppermute | solution.py:44
  152.0 19.5 %collective-permute-start.26 = (bf16[256,256]{1,0:T(8,128)(2,1)S(1)}, bf16[256,256]{1,0:T(8,128)(2,1)S(1)}, u32[]{:S(2)}, u32[]{:S(2)}) collective-permute-start(bf16[256,256]{1,0:T(8,128)(2,1)S(1)} %collective-permute-done.24), channel_id=1, source_target_pairs={{0,15},{1,0},{2,1},{3,2},{4,3},{5,4},{6,5},{7,6},{8,7},{9,8},{10,9... | collective-permute-start | bytes 393224 | tf_op jit(solution)/shard_map/ppermute | solution.py:44
  158.8 18.8 %collective-permute-start.11 = (bf16[256,256]{1,0:T(8,128)(2,1)S(1)}, bf16[256,256]{1,0:T(8,128)(2,1)S(1)}, u32[]{:S(2)}, u32[]{:S(2)}) collective-permute-start(bf16[256,256]{1,0:T(8,128)(2,1)S(1)} %collective-permute-done.9), channel_id=1, source_target_pairs={{0,15},{1,0},{2,1},{3,2},{4,3},{5,4},{6,5},{7,6},{8,7},{9,8},{10,9... | collective-permute-start | bytes 393224 | tf_op jit(solution)/shard_map/ppermute | solution.py:44
  171.5 18.8 %collective-permute-start.56 = (bf16[256,256]{1,0:T(8,128)(2,1)S(1)}, bf16[256,256]{1,0:T(8,128)(2,1)S(1)}, u32[]{:S(2)}, u32[]{:S(2)}) collective-permute-start(bf16[256,256]{1,0:T(8,128)(2,1)S(1)} %collective-permute-done.54), channel_id=1, source_target_pairs={{0,15},{1,0},{2,1},{3,2},{4,3},{5,4},{6,5},{7,6},{8,7},{9,8},{10,9... | collective-permute-start | bytes 393224 | tf_op jit(solution)/shard_map/ppermute | solution.py:44
  177.6 49.6 %collective-permute-start.28 = (bf16[256,256]{1,0:T(8,128)(2,1)S(1)}, bf16[256,256]{1,0:T(8,128)(2,1)}, u32[]{:S(2)}, u32[]{:S(2)}) collective-permute-start(bf16[256,256]{1,0:T(8,128)(2,1)S(1)} %collective-permute-done.26), channel_id=1, source_target_pairs={{0,15},{1,0},{2,1},{3,2},{4,3},{5,4},{6,5},{7,6},{8,7},{9,8},{10,9... | collective-permute-start | bytes 393224 | tf_op jit(solution)/shard_map/ppermute | solution.py:44
  184.3 23.4 %collective-permute-start.13 = (bf16[256,256]{1,0:T(8,128)(2,1)S(1)}, bf16[256,256]{1,0:T(8,128)(2,1)S(1)}, u32[]{:S(2)}, u32[]{:S(2)}) collective-permute-start(bf16[256,256]{1,0:T(8,128)(2,1)S(1)} %collective-permute-done.11), channel_id=1, source_target_pairs={{0,15},{1,0},{2,1},{3,2},{4,3},{5,4},{6,5},{7,6},{8,7},{9,8},{10,9... | collective-permute-start | bytes 393224 | tf_op jit(solution)/shard_map/ppermute | solution.py:44
  191.0 108.4 %collective-permute-start.43 = (bf16[256,256]{1,0:T(8,128)(2,1)S(1)}, bf16[256,256]{1,0:T(8,128)(2,1)}, u32[]{:S(2)}, u32[]{:S(2)}) collective-permute-start(bf16[256,256]{1,0:T(8,128)(2,1)S(1)} %collective-permute-done.41), channel_id=1, source_target_pairs={{0,15},{1,0},{2,1},{3,2},{4,3},{5,4},{6,5},{7,6},{8,7},{9,8},{10,9... | collective-permute-start | bytes 393224 | tf_op jit(solution)/shard_map/ppermute | solution.py:44
  200.1 169.7 %collective-permute-start.58 = (bf16[256,256]{1,0:T(8,128)(2,1)S(1)}, bf16[256,256]{1,0:T(8,128)(2,1)S(1)}, u32[]{:S(2)}, u32[]{:S(2)}) collective-permute-start(bf16[256,256]{1,0:T(8,128)(2,1)S(1)} %collective-permute-done.56), channel_id=1, source_target_pairs={{0,15},{1,0},{2,1},{3,2},{4,3},{5,4},{6,5},{7,6},{8,7},{9,8},{10,9... | collective-permute-start | bytes 393224 | tf_op jit(solution)/shard_map/ppermute | solution.py:44
  207.7 20.5 %collective-permute-start.29 = (bf16[256,256]{1,0:T(8,128)(2,1)}, bf16[256,256]{1,0:T(8,128)(2,1)}, u32[]{:S(2)}, u32[]{:S(2)}) collective-permute-start(bf16[256,256]{1,0:T(8,128)(2,1)} %collective-permute-done.27), channel_id=1, source_target_pairs={{0,1},{1,2},{2,3},{3,4},{4,5},{5,6},{6,7},{7,8},{8,9},{9,10},{10,1... | collective-permute-start | bytes 393224 | tf_op jit(solution)/shard_map/ppermute | solution.py:37
  215.3 85.6 %collective-permute-start.44 = (bf16[256,256]{1,0:T(8,128)(2,1)}, bf16[256,256]{1,0:T(8,128)(2,1)}, u32[]{:S(2)}, u32[]{:S(2)}) collective-permute-start(bf16[256,256]{1,0:T(8,128)(2,1)} %collective-permute-done.42), channel_id=1, source_target_pairs={{0,1},{1,2},{2,3},{3,4},{4,5},{5,6},{6,7},{7,8},{8,9},{9,10},{10,1... | collective-permute-start | bytes 393224 | tf_op jit(solution)/shard_map/ppermute | solution.py:37
  227.1 131.9 %all-reduce.9.cloned.1.call-start = ((), (), s32[]{:S(2)}) async-start(), calls=%async_computation.2 | async-start | bytes 786432 | tf_op jit(solution)/shard_map/psum | solution.py:9
  227.2 143.3 %collective-permute-start.59 = (bf16[256,256]{1,0:T(8,128)(2,1)S(1)}, bf16[256,256]{1,0:T(8,128)(2,1)S(1)}, u32[]{:S(2)}, u32[]{:S(2)}) collective-permute-start(bf16[256,256]{1,0:T(8,128)(2,1)S(1)} %collective-permute-done.57), channel_id=1, source_target_pairs={{0,1},{1,2},{2,3},{3,4},{4,5},{5,6},{6,7},{7,8},{8,9},{9,10},{10,1... | collective-permute-start | bytes 393224 | tf_op jit(solution)/shard_map/ppermute | solution.py:37
  299.1 130.6 %all-reduce.11.cloned.1.call-start = ((), (), s32[]{:S(2)}) async-start(), calls=%async_computation.3 | async-start | bytes 786432 | tf_op jit(solution)/shard_map/psum | solution.py:9
  (40 other events, 479.4 us)
Sparse Core Ops, SparseCore 0:
  22.4 57.4 all-reduce.4
  227.2 61.6 all-reduce.6
  299.2 59.7 all-reduce.8
  369.9 59.7 all-reduce.10
